TPU v7x, 128 devices: a whole 4x4x4 slice. The times are simulated.
128 devices in a mesh: gx: 16 (over z, x_hi, core), gy: 8 (over x_lo, y).
Axes of the slice: x: 4 (x_hi: 2, x_lo: 2; x = x_hi * 2 + x_lo), y: 4, z: 4, core: 2. Of those that a mesh axis runs over, the one named last changes fastest.
Arguments:
- grid_field: bfloat16 [1, 20, 2048, 2048], P(None, None, 'gx', 'gy'), may hold values from -8 to 8
- spectral_weight: float32 [2, 2, 20, 20, 2048], P(None, None, None, None, ('gx', 'gy')), may hold values from -1 to 1
- conv_near: bfloat16 [2, 20, 180], replicated, may hold values from -0.4375 to 0.4375
- conv_far: bfloat16 [2, 20, 500], replicated, may hold values from -0.25 to 0.25
- mix_logits: float32 [2, 3], replicated, may hold values from -1 to 1
- channel_bias: float32 [2, 20], replicated, may hold values from -3 to 3
Outputs:
- result_field: bfloat16 [1, 20, 2048, 2048], P(None, None, 'gx', 'gy')
All inputs are finite; a program needn't handle non-finite values.
Results may differ from a plain program's by a relative error of at most 0.004.
Values may be sent and summed in bfloat16 or wider, within the bound.
No kernel may reach another device: no remote copies, remote signals or barrier semaphores. Data moves between devices by JAX's collectives and lax.ppermute only.
A program may use at most 192 MiB of HBM per device.

v0:
```python
import math
import jax
import jax.numpy as jnp
from jax import lax
from jax.sharding import PartitionSpec as P

NX = 2048
NY = 2048
MX = 32
MY = 32
LAYERS = 2
KX = 64
MODES = 2048
full_turn = 2.0 * math.pi
highest = lax.Precision.HIGHEST


def padded_2(value, sides, width):
    for axis, dim in sides:
        size, length = (lax.axis_size(axis), value.shape[dim])
        up = [(i, (i + 1) % size) for i in range(size)]
        down = [(j, i) for i, j in up]
        last = lax.slice_in_dim(value, length - width, length, axis=dim)
        first = lax.slice_in_dim(value, 0, width, axis=dim)
        before = lax.ppermute(last, axis, up)
        after = lax.ppermute(first, axis, down)
        value = jnp.concatenate([before, value, after], axis=dim)
    return value


def forward_table(positions):
    col_modes = jnp.arange(MY, dtype=jnp.int32)
    phases = (positions[:, None] * col_modes[None, :] % NY).astype(jnp.float32) * (full_turn / NY)
    return jnp.concatenate([jnp.cos(phases), -jnp.sin(phases)], axis=1).astype(jnp.bfloat16)


def row_tables(positions):
    lower = jnp.arange(MX, dtype=jnp.int32)
    row_modes = jnp.concatenate([lower, lower + (NX - MX)])
    phases = (positions[:, None] * row_modes[None, :] % NX).astype(jnp.float32) * (full_turn / NX)
    return (jnp.cos(phases), jnp.sin(phases))


def inverse_table(positions):
    col_modes = jnp.arange(MY, dtype=jnp.int32)
    col_weight = jnp.where(col_modes == 0, 1.0, 2.0).astype(jnp.float32) / (NX * NY)
    phases = (col_modes[:, None] * positions[None, :] % NY).astype(jnp.float32) * (full_turn / NY)
    return jnp.concatenate(
        [jnp.cos(phases) * col_weight[:, None], -jnp.sin(phases) * col_weight[:, None]], axis=0
    )


def conv_rows(padded_plane, tap_weights, dilation, side_taps, first_row, count_rows, local_cols):
    channels = padded_plane.shape[0]
    pieces = []
    for row_tap in range(side_taps):
        for col_tap in range(side_taps):
            row_offset = 4 + (row_tap - side_taps // 2) * dilation + first_row
            col_offset = 4 + (col_tap - side_taps // 2) * dilation
            pieces.append(
                padded_plane[
                    :, row_offset : row_offset + count_rows, col_offset : col_offset + local_cols
                ]
            )
    stacked = jnp.stack(pieces, 0)
    shaped_weights = tap_weights.reshape(channels, side_taps * side_taps, channels)
    return jnp.einsum("otc,tcxy->oxy", shaped_weights, stacked, preferred_element_type=jnp.float32)


def on_device(grid_field, spectral_weight, conv_near, conv_far, mix_logits, channel_bias):
    channels = grid_field.shape[1]
    local_rows = grid_field.shape[2]
    local_cols = grid_field.shape[3]
    row_positions = lax.axis_index("gx") * local_rows + jnp.arange(local_rows, dtype=jnp.int32)
    col_positions = lax.axis_index("gy") * local_cols + jnp.arange(local_cols, dtype=jnp.int32)
    forward_cols = forward_table(col_positions)
    cosine_rows, sine_rows = row_tables(row_positions)
    inverse_cols = inverse_table(col_positions)
    share_modes = spectral_weight.shape[-1]
    owner_index = lax.axis_index("gx") * lax.axis_size("gy") + lax.axis_index("gy")
    mode_start = owner_index * share_modes
    row_blocks = max(1, local_rows // 32)
    while local_rows % row_blocks != 0:
        row_blocks = row_blocks - 1
    block_rows = local_rows // row_blocks
    planes_block = grid_field
    for layer_index in range(LAYERS):
        planes_here = planes_block.shape[0]
        line_sums = jnp.dot(
            planes_block.reshape(planes_here * channels * local_rows, local_cols),
            forward_cols,
            preferred_element_type=jnp.float32,
        )
        line_sums = line_sums.reshape(planes_here, channels, local_rows, 2 * MY)
        real_lines = line_sums[..., :MY]
        imaginary_lines = line_sums[..., MY:]

        def contract_rows(operand, lookup):
            return jnp.einsum("pcxk,xj->pcjk", operand, lookup, precision=highest)

        real_spec = contract_rows(real_lines, cosine_rows) + contract_rows(
            imaginary_lines, sine_rows
        )
        imaginary_spec = contract_rows(imaginary_lines, cosine_rows) - contract_rows(
            real_lines, sine_rows
        )
        partial_value = jnp.stack(
            [
                real_spec.reshape(planes_here, channels, MODES),
                imaginary_spec.reshape(planes_here, channels, MODES),
            ]
        )
        totals = lax.psum(partial_value, ("gx", "gy"))
        own_modes = lax.dynamic_slice_in_dim(totals, mode_start, share_modes, 3)

        def mix_modes(spectrum, weights):
            return jnp.einsum("pcm,com->pom", spectrum, weights, precision=highest)

        weight_real = spectral_weight[layer_index, 0]
        weight_imaginary = spectral_weight[layer_index, 1]
        real_mixed = mix_modes(own_modes[0], weight_real) - mix_modes(
            own_modes[1], weight_imaginary
        )
        imaginary_mixed = mix_modes(own_modes[1], weight_real) + mix_modes(
            own_modes[0], weight_imaginary
        )
        own_block = jnp.stack([real_mixed, imaginary_mixed])[None]
        gathered = lax.all_gather(own_block, ("gx", "gy"), axis=0, tiled=True)
        gathered = jnp.transpose(gathered, (1, 2, 3, 0, 4)).reshape(2, planes_here, channels, MODES)
        real_full = gathered[0].reshape(planes_here, channels, KX, MY)
        imaginary_full = gathered[1].reshape(planes_here, channels, KX, MY)

        def expand_rows(spectrum, lookup):
            return jnp.einsum("pcjk,xj->pcxk", spectrum, lookup, precision=highest)

        real_rows = expand_rows(real_full, cosine_rows) - expand_rows(imaginary_full, sine_rows)
        imaginary_rows = expand_rows(real_full, sine_rows) + expand_rows(
            imaginary_full, cosine_rows
        )
        stacked = jnp.concatenate([real_rows, imaginary_rows], axis=-1).reshape(
            planes_here * channels * local_rows, 2 * MY
        )
        spectral = jnp.dot(stacked, inverse_cols, precision=highest)
        layer_spectral = spectral.reshape(planes_here, channels, local_rows, local_cols)
        padded = padded_2(planes_block, (("gx", 2), ("gy", 3)), 4)
        exponents = jnp.exp(mix_logits[layer_index])
        mixture = exponents / jnp.sum(exponents)
        bias_column = channel_bias[layer_index][:, None, None]
        row_pieces = []
        for block_index in range(row_blocks):
            first_row = block_index * block_rows
            near_term = conv_rows(
                padded[0], conv_near[layer_index], 1, 3, first_row, block_rows, local_cols
            )
            far_term = conv_rows(
                padded[0], conv_far[layer_index], 2, 5, first_row, block_rows, local_cols
            )
            spectral_rows = layer_spectral[0, :, first_row : first_row + block_rows, :]
            summed = (
                mixture[0] * spectral_rows
                + mixture[1] * near_term
                + mixture[2] * far_term
                + bias_column
            )
            row_pieces.append(jax.nn.gelu(summed, approximate=False).astype(jnp.bfloat16))
        outputs = [jnp.concatenate(row_pieces, axis=1)]
        planes_block = jnp.stack(outputs)
    return planes_block


def solution(mesh):
    in_specs = (
        P(None, None, "gx", "gy"),
        P(None, None, None, None, ("gx", "gy")),
        P(),
        P(),
        P(),
        P(),
    )
    out_specs = P(None, None, "gx", "gy")
    return jax.shard_map(
        on_device, mesh=mesh, in_specs=in_specs, out_specs=out_specs, check_vma=False
    )
```

profile of v0, /device:TPU:0, one launch (start us, length us, event | category | flops | bytes accessed | tf_op | source)
XLA Modules:
  0.0 1025.7 jit_solution(15079216024907753427)
XLA Ops:
  8.8 6.0 collective-permute-start.1
  15.0 1.9 convolution_bitcast_fusion
  23.0 2.0 slice_bitcast_fusion.263
  27.7 2.0 broadcast_divide_fusion.1
  37.3 2.9 collective-permute-start.3
  40.8 1.7 reshape_squeeze.9
  71.0 3.8 copy-done.15
  74.8 14.7 %constant_dynamic-update-slice_fusion.20 = (bf16[25,20,32,256]{3,1,2,0:T(8,128)(2,1)}, bf16[25,20,32,256]{3,1,2,0:T(8,128)(2,1)S(1)}, bf16[9,20,32,256]{3,1,2,0:...) fusion(bf16[25,20,32,256]{3,1,2,0:T(8,128)(2,1)} %get-tuple-ele, ...), kind=kLoop, calls=%fused_computation.275 | loop fusion | bytes 5505024
  89.7 1.9 constant_dynamic-update-slice_fusion.19
  91.6 1.9 constant_dynamic-update-slice_fusion.18
  93.4 1.7 constant_dynamic-update-slice_fusion.17
  96.6 1.9 constant_dynamic-update-slice_fusion.15
  98.5 1.8 constant_dynamic-update-slice_fusion.14
  100.3 1.8 constant_dynamic-update-slice_fusion.13
  104.6 2.3 convolution_bitcast_fusion.3
  106.9 2.4 convolution_bitcast_fusion.5
  109.3 6.5 convolution_bitcast_fusion.7
  115.8 2.3 convolution_bitcast_fusion.9
  124.9 39.9 %all-reduce.3.cloned.1.call-done = f32[2,1,20,2048]{3,0,2,1:T(2,128)} async-done(((f32[2,1,20,2048]{3,0,2,1:T(2,128)}), f32[2,1,20,2048]{3,0,2,1:T(2,128)}) %all-reduce.3.cloned.1.call-update) | async-done | bytes 327696 | tf_op jit(solution)/shard_map/psum | solution.py:113
  167.1 326.2 %all-gather = f32[256,1,20,16]{2,3,1,0:T(8,128)S(1)} all-gather(f32[2,1,20,16]{2,3,1,0:T(8,128)S(1)} %pad_maximum_fusion.8), channel_id=2, replica_groups=mesh['gx'=16,'gy'=8] {'gx','gy'}, dimensions={0}, use_global_device_ids=true | all-gather | bytes 330240 | tf_op jit(solution)/shard_map/all_gather | solution.py:128
  500.9 2.2 convolution_bitcast_fusion.2
  503.2 10.4 %fusion.42 = (bf16[20,32,256]{2,1,0:T(8,128)(2,1)S(1)}, bf16[20,32,256]{2,1,0:T(8,128)(2,1)S(1)}, bf16[20,32,256]{2,1,0:T(8,128)(2,1)S(1)}, bf16[20,32,256]{2,1,0:T(8,128)(2,1)S(1)}) fusion(f32[32,256,20]{1,2,0:T(8,128)} %convolution_bitcast_fusion.9, f32[32,256,20]{1,2,0:T(8,128)} %convolution_bitcast_fusion.10, ...), kind=kLoop, calls=%fused_computation.51 | loop fusion | flops 46530560 | bytes 9175132 | tf_op jit(solution)/shard_map/convert_element_type | solution.py:165
  516.9 5.3 collective-permute-start.5
  526.1 4.3 collective-permute-start.7
  532.6 1.8 maximum_bitcast_fusion.1
  548.7 3.2 copy-done.18
  552.0 2.1 constant_dynamic-update-slice_fusion.147
  554.4 2.9 constant_dynamic-update-slice_fusion.146
  557.2 2.7 constant_dynamic-update-slice_fusion.145
  560.0 2.6 constant_dynamic-update-slice_fusion.144
  562.6 2.9 constant_dynamic-update-slice_fusion.143
  565.5 2.6 constant_dynamic-update-slice_fusion.142
  568.1 2.6 constant_dynamic-update-slice_fusion.141
  570.7 2.6 constant_dynamic-update-slice_fusion.140
  573.2 2.5 constant_dynamic-update-slice_fusion.139
  576.2 2.8 copy-done.16
  579.2 4.5 fusion.25
  583.7 9.6 fusion.19
  593.3 5.3 fusion.22
  598.6 5.3 fusion.16
  603.8 2.6 fusion.28
  606.4 2.8 fusion.31
  609.2 2.6 fusion.34
  611.7 2.6 fusion.37
  614.3 58.0 %all-reduce.5.cloned.1.call-done = f32[2,1,20,2048]{3,0,2,1:T(2,128)} async-done(((f32[2,1,20,2048]{3,0,2,1:T(2,128)}), f32[2,1,20,2048]{3,0,2,1:T(2,128)}) %all-reduce.5.cloned.1.call-update) | async-done | bytes 327696 | tf_op jit(solution)/shard_map/psum | solution.py:113
  674.7 325.8 %all-gather.1 = f32[256,1,20,16]{2,3,1,0:T(8,128)S(1)} all-gather(f32[2,1,20,16]{2,3,1,0:T(8,128)S(1)} %pad_maximum_fusion.9), channel_id=3, replica_groups=mesh['gx'=16,'gy'=8] {'gx','gy'}, dimensions={0}, use_global_device_ids=true | all-gather | bytes 330240 | tf_op jit(solution)/shard_map/all_gather | solution.py:128
  1004.6 2.2 convolution_bitcast_fusion.1
  1006.8 10.5 %fusion.54 = (bf16[20,32,256]{2,1,0:T(8,128)(2,1)S(1)}, bf16[20,32,256]{2,1,0:T(8,128)(2,1)S(1)}, bf16[20,32,256]{2,1,0:T(8,128)(2,1)S(1)}, bf16[20,32,256]{2,1,0:T(8,128)(2,1)S(1)}) fusion(f32[32,256,20]{1,2,0:T(8,128)} %fusion.16, f32[32,256,20]{1,2,0:T(8,128)} %fusion.28, f32[1,20,128,256]{3,2,1,0:T(8,128)S(1)} %convolution_bitcast_fusion.1, ...), kind=kLoop, calls=%fused_computation.63 | loop fusion | flops 46530560 | bytes 9175132 | tf_op jit(solution)/shard_map/convert_element_type | solution.py:165
  (225 shorter events, 100.2 us)
Async XLA Ops:
  6.5 15.6 %copy-start.8 = (bf16[2,20,500]{2,0,1:T(2,128)(2,1)S(1)}, bf16[2,20,500]{2,0,1:T(2,128)(2,1)}, u32[]{:S(2)}) copy-start(bf16[2,20,500]{2,0,1:T(2,128)(2,1)} %param.9) | copy-start | bytes 120004
  6.5 158.2 %all-reduce.3.cloned.1.call-start = ((), (), s32[]{:S(2)}) async-start(), calls=%async_computation | async-start | bytes 655360 | tf_op jit(solution)/shard_map/psum | solution.py:113
  8.1 23.0 %collective-permute-start = (bf16[1,20,4,256]{3,1,2,0:T(8,128)(2,1)}, bf16[1,20,4,256]{3,1,2,0:T(8,128)(2,1)}, u32[]{:S(2)}, u32[]{:S(2)}) collective-permute-start(bf16[1,20,4,256]{3,1,2,0:T(8,128)(2,1)} %copy.500), channel_id=1, source_target_pairs={{0,8},{8,16},{16,24},{24,32},{32,40},{40,48},{48,56},{56,64},{64,7... | collective-permute-start | bytes 122888 | tf_op jit(solution)/shard_map/ppermute | solution.py:25
  8.8 24.0 %collective-permute-start.1 = (bf16[1,20,4,256]{3,1,2,0:T(8,128)(2,1)}, bf16[1,20,4,256]{3,1,2,0:T(8,128)(2,1)}, u32[]{:S(2)}, u32[]{:S(2)}) collective-permute-start(bf16[1,20,4,256]{3,1,2,0:T(8,128)(2,1)} %copy.501), channel_id=1, source_target_pairs={{8,0},{16,8},{24,16},{32,24},{40,32},{48,40},{56,48},{64,56},{72,6... | collective-permute-start | bytes 122888 | tf_op jit(solution)/shard_map/ppermute | solution.py:26
  15.0 7.2 copy-start.11
  15.0 7.2 copy-start.13
  15.0 10.7 %copy-start.19 = (f32[2,3]{1,0:T(2,128)S(1)}, f32[2,3]{1,0:T(2,128)}, u32[]{:S(2)}) copy-start(f32[2,3]{1,0:T(2,128)} %param.10) | copy-start | bytes 76
  15.0 17.0 %copy-start = (bf16[1,20,128,256]{3,2,1,0:T(8,128)(2,1)S(1)}, bf16[1,20,128,256]{3,2,1,0:T(8,128)(2,1)}, u32[]{:S(2)}) copy-start(bf16[1,20,128,256]{3,2,1,0:T(8,128)(2,1)} %param.6) | copy-start | bytes 3932164
  22.1 650.2 %all-reduce.5.cloned.1.call-start = ((), (), s32[]{:S(2)}) async-start(), calls=%async_computation.1 | async-start | bytes 655360 | tf_op jit(solution)/shard_map/psum | solution.py:113
  35.1 12.2 %collective-permute-start.2 = (bf16[1,20,136,4]{2,3,1,0:T(4,128)(2,1)}, bf16[1,20,136,4]{2,3,1,0:T(4,128)(2,1)S(1)}, u32[]{:S(2)}, u32[]{:S(2)}) collective-permute-start(bf16[1,20,136,4]{2,3,1,0:T(4,128)(2,1)} %copy.211), channel_id=1, source_target_pairs={{0,1},{1,2},{2,3},{3,4},{4,5},{5,6},{6,7},{7,0},{8,9},{9,10},{10,1... | collective-permute-start | bytes 65288 | tf_op jit(solution)/shard_map/ppermute | solution.py:25
  37.3 10.6 %collective-permute-start.3 = (bf16[1,20,136,4]{2,3,1,0:T(4,128)(2,1)S(1)}, bf16[1,20,136,4]{2,3,1,0:T(4,128)(2,1)}, u32[]{:S(2)}, u32[]{:S(2)}) collective-permute-start(bf16[1,20,136,4]{2,3,1,0:T(4,128)(2,1)S(1)} %copy.212), channel_id=1, source_target_pairs={{1,0},{2,1},{3,2},{4,3},{5,4},{6,5},{7,6},{0,7},{9,8},{10,9},{11,1... | collective-permute-start | bytes 65288 | tf_op jit(solution)/shard_map/ppermute | solution.py:26
  71.0 3.8 copy-start.15
  100.3 4.3 copy-start.7
  106.9 8.9 slice-start
  106.9 8.9 slice-start.1
  109.3 6.5 slice-start.2
  115.8 2.4 copy-start.5
  120.4 45.4 %copy-start.4 = (f32[20,20,16]{1,2,0:T(8,128)S(1)}, f32[20,20,16]{1,2,0:T(8,128)}, u32[]{:S(2)}) copy-start(f32[20,20,16]{1,2,0:T(8,128)} %get-tuple-element.287) | copy-start | bytes 76804
  120.4 46.1 %copy-start.3 = (f32[20,20,16]{1,2,0:T(8,128)S(1)}, f32[20,20,16]{1,2,0:T(8,128)}, u32[]{:S(2)}) copy-start(f32[20,20,16]{1,2,0:T(8,128)} %get-tuple-element.286) | copy-start | bytes 76804
  124.9 376.1 %copy-start.6 = (f32[32,256]{1,0:T(8,128)S(1)}, f32[32,256]{1,0:T(8,128)}, u32[]{:S(2)}) copy-start(f32[32,256]{1,0:T(8,128)} %get-tuple-element.296) | copy-start | bytes 98308
  167.1 336.1 %copy-start.21 = (f32[20]{0:T(128)S(1)}, f32[20]{0:T(128)}, u32[]{:S(2)}) copy-start(f32[20]{0:T(128)} %get-tuple-element.300) | copy-start | bytes 244
  494.2 9.0 copy-start.1
  500.9 12.8 %copy-start.12 = (bf16[256,32]{0,1:T(8,128)(2,1)S(1)}, bf16[256,32]{0,1:T(8,128)(2,1)}, u32[]{:S(2)}) copy-start(bf16[256,32]{0,1:T(8,128)(2,1)} %copy-done.11) | copy-start | bytes 49156
  500.9 12.8 %copy-start.14 = (bf16[256,32]{0,1:T(8,128)(2,1)S(1)}, bf16[256,32]{0,1:T(8,128)(2,1)}, u32[]{:S(2)}) copy-start(bf16[256,32]{0,1:T(8,128)(2,1)} %copy-done.13) | copy-start | bytes 49156
  516.8 7.1 collective-permute-start.4
  516.9 7.0 collective-permute-start.5
  525.6 6.2 collective-permute-start.6
  526.1 6.0 collective-permute-start.7
  548.7 3.2 copy-start.18
  568.1 11.1 %copy-start.9 = (bf16[20,25,20]{1,0,2:T(8,128)(2,1)S(1)}, bf16[20,25,20]{1,0,2:T(8,128)(2,1)}, u32[]{:S(2)}) copy-start(bf16[20,25,20]{1,0,2:T(8,128)(2,1)} %copy.257) | copy-start | bytes 60004
  575.7 3.3 copy-start.16
  583.7 9.6 copy-start.17
  598.6 5.3 copy-start.10
  606.4 66.9 %copy-start.2 = (f32[20,20,16]{1,2,0:T(8,128)S(1)}, f32[20,20,16]{1,2,0:T(8,128)}, u32[]{:S(2)}) copy-start(f32[20,20,16]{1,2,0:T(8,128)} %get-tuple-element.285) | copy-start | bytes 76804
  674.7 332.2 %copy-start.20 = (f32[20]{0:T(128)S(1)}, f32[20]{0:T(128)}, u32[]{:S(2)}) copy-start(f32[20]{0:T(128)} %get-tuple-element.299) | copy-start | bytes 244
Sparse Core Ops, SparseCore 0:
  22.2 142.4 all-reduce.2
  531.7 140.5 all-reduce.4
where the time goes:
time: 1030 us
  blocking collectives  652 us (63%)
  local copies, waits for them, and re-layouts  131 us (13%)
  waiting for transfers between devices  98.6 us (10%)
  matrix products  74.6 us (7%)
  other arithmetic  34.5 us (3%)
  starting transfers between devices  20.3 us (2%)
  between operations  14.7 us (1%)
    all_gather x2, blocking collectives, on_device(): gathered = lax.all_gather(own_block, ('gx', 'gy'), axis=0, tiled=True)  652 us
    unnamed x121, local copies, waits for them, and re-layouts  98.1 us
    psum x2, waiting for transfers between devices, on_device(): totals = lax.psum(partial_value, ('gx', 'gy'))  97.8 us
    dot_general x16, matrix products, conv_rows(): jnp.einsum('otc,tcxy->oxy', shaped_weights, stacked, preferred_element_ty...  53.9 us
    convert_element_type x2, other arithmetic, on_device(): jax.nn.gelu(summed, approximate=False).astype(jnp.bfloat16)  20.9 us
  transfers between devices with their start and end apart: 10, of which 4 were waited for; matrix products, arithmetic and copies ran while one was open for 18% of the time, Pallas kernels for 0%

commit v1 on v0

--- a/solution.py
+++ b/solution.py
@@ -110,7 +110,7 @@
                 imaginary_spec.reshape(planes_here, channels, MODES),
             ]
         )
-        totals = lax.psum(partial_value, ("gx", "gy"))
+        totals = lax.psum(lax.psum(partial_value, "gy"), "gx")
         own_modes = lax.dynamic_slice_in_dim(totals, mode_start, share_modes, 3)
 
         def mix_modes(spectrum, weights):

time: 1030 us -> 1200 us (1.17)
  waiting for transfers between devices: 98.6 us -> 259 us
    psum x2 -> x4, waiting for transfers between devices: 97.8 us -> 258 us  [on_device(): totals = lax.psum(lax.psum(partial_value, 'gy'), 'gx')]
  transfers between devices with their start and end apart: 10 -> 12, of which waited for: 4 -> 4; matrix products, arithmetic and copies ran while one was open for 18% -> 15% of each run, Pallas kernels for 0% -> 0%
where the time goes in v1:
time: 1200 us
  blocking collectives  654 us (54%)
  waiting for transfers between devices  259 us (22%)
  local copies, waits for them, and re-layouts  131 us (11%)
  matrix products  82.2 us (7%)
  other arithmetic  35.4 us (3%)
  starting transfers between devices  20.5 us (2%)
  between operations  14.4 us (1%)
    all_gather x2, blocking collectives, on_device(): gathered = lax.all_gather(own_block, ('gx', 'gy'), axis=0, tiled=True)  654 us
    psum x4, waiting for transfers between devices, on_device(): totals = lax.psum(lax.psum(partial_value, 'gy'), 'gx')  258 us
    unnamed x121, local copies, waits for them, and re-layouts  105 us
    dot_general x16, matrix products, conv_rows(): jnp.einsum('otc,tcxy->oxy', shaped_weights, stacked, preferred_element_ty...  57.8 us
  transfers between devices with their start and end apart: 12, of which 4 were waited for; matrix products, arithmetic and copies ran while one was open for 15% of the time, Pallas kernels for 0%

profile of v1, /device:TPU:0, one launch (start us, length us, event | category | flops | bytes accessed | tf_op | source)
XLA Modules:
  0.0 1197.0 jit_solution(9901035470361813154)
XLA Ops:
  8.8 6.0 collective-permute-start.1
  15.0 1.9 convolution_bitcast_fusion
  22.4 2.0 slice_bitcast_fusion.263
  32.4 2.9 collective-permute-start.3
  41.6 3.2 maximum_bitcast_fusion
  65.8 3.8 copy-done.16
  69.6 14.6 %constant_dynamic-update-slice_fusion.20 = (bf16[25,20,32,256]{3,1,2,0:T(8,128)(2,1)}, bf16[25,20,32,256]{3,1,2,0:T(8,128)(2,1)S(1)}, bf16[9,20,32,256]{3,1,2,0:...) fusion(bf16[25,20,32,256]{3,1,2,0:T(8,128)(2,1)} %get-tuple-ele, ...), kind=kLoop, calls=%fused_computation.275 | loop fusion | bytes 5505024
  84.5 1.9 constant_dynamic-update-slice_fusion.19
  86.3 1.9 constant_dynamic-update-slice_fusion.18
  88.2 1.7 constant_dynamic-update-slice_fusion.17
  91.4 1.9 constant_dynamic-update-slice_fusion.15
  93.3 1.8 constant_dynamic-update-slice_fusion.14
  95.1 1.8 constant_dynamic-update-slice_fusion.13
  99.3 2.4 convolution_bitcast_fusion.3
  101.7 2.4 convolution_bitcast_fusion.5
  104.2 6.4 convolution_bitcast_fusion.7
  110.6 2.3 convolution_bitcast_fusion.9
  124.5 3.5 convolution_bitcast_fusion.10
  128.0 127.9 %all-reduce.7.cloned.1.call-done = f32[2,1,20,2048]{3,0,2,1:T(2,128)} async-done(((f32[2,1,20,2048]{3,0,2,1:T(2,128)}), f32[2,1,20,2048]{3,0,2,1:T(2,128)}) %all-reduce.7.cloned.1.call-update) | async-done | bytes 327696 | tf_op jit(solution)/shard_map/psum | solution.py:113
  262.0 327.5 %all-gather = f32[256,1,20,16]{2,3,1,0:T(8,128)S(1)} all-gather(f32[2,1,20,16]{2,3,1,0:T(8,128)S(1)} %pad_maximum_fusion.8), channel_id=2, replica_groups=mesh['gx'=16,'gy'=8] {'gx','gy'}, dimensions={0}, use_global_device_ids=true | all-gather | bytes 330240 | tf_op jit(solution)/shard_map/all_gather | solution.py:128
  597.1 2.2 convolution_bitcast_fusion.2
  599.3 10.3 fusion.42
  612.9 5.3 collective-permute-start.5
  622.2 4.2 collective-permute-start.7
  628.7 1.8 maximum_bitcast_fusion.1
  644.8 3.2 copy-done.19
  648.0 2.1 constant_dynamic-update-slice_fusion.147
  650.4 2.9 constant_dynamic-update-slice_fusion.146
  653.3 2.7 constant_dynamic-update-slice_fusion.145
  656.0 2.6 constant_dynamic-update-slice_fusion.144
  658.7 2.9 constant_dynamic-update-slice_fusion.143
  661.6 2.6 constant_dynamic-update-slice_fusion.142
  664.2 2.6 constant_dynamic-update-slice_fusion.141
  666.7 2.6 constant_dynamic-update-slice_fusion.140
  669.3 2.5 constant_dynamic-update-slice_fusion.139
  672.3 2.8 copy-done.17
  675.2 4.5 fusion.25
  679.8 9.6 fusion.19
  689.4 5.3 fusion.22
  694.6 5.3 fusion.16
  699.9 2.6 fusion.28
  702.5 2.8 fusion.31
  705.2 2.6 fusion.34
  707.8 4.4 fusion.37
  712.2 130.4 %all-reduce.11.cloned.1.call-done = f32[2,1,20,2048]{3,0,2,1:T(2,128)} async-done(((f32[2,1,20,2048]{3,0,2,1:T(2,128)}), f32[2,1,20,2048]{3,0,2,1:T(2,128)}) %all-reduce.11.cloned.1.call-update) | async-done | bytes 327696 | tf_op jit(solution)/shard_map/psum | solution.py:113
  845.1 327.0 %all-gather.1 = f32[256,1,20,16]{2,3,1,0:T(8,128)S(1)} all-gather(f32[2,1,20,16]{2,3,1,0:T(8,128)S(1)} %pad_maximum_fusion.9), channel_id=3, replica_groups=mesh['gx'=16,'gy'=8] {'gx','gy'}, dimensions={0}, use_global_device_ids=true | all-gather | bytes 330240 | tf_op jit(solution)/shard_map/all_gather | solution.py:128
  1176.2 2.2 convolution_bitcast_fusion.1
  1178.4 10.5 fusion.54
  (231 shorter events, 104.2 us)
Async XLA Ops:
  6.5 15.7 %copy-start.7 = (bf16[2,20,500]{2,0,1:T(2,128)(2,1)S(1)}, bf16[2,20,500]{2,0,1:T(2,128)(2,1)}, u32[]{:S(2)}) copy-start(bf16[2,20,500]{2,0,1:T(2,128)(2,1)} %param.9) | copy-start | bytes 120004
  6.5 117.0 %all-reduce.5.cloned.1.call-start = ((), (), s32[]{:S(2)}) async-start(), calls=%async_computation | async-start | bytes 655360 | tf_op jit(solution)/shard_map/psum | solution.py:113
  8.1 19.1 %collective-permute-start = (bf16[1,20,4,256]{3,1,2,0:T(8,128)(2,1)}, bf16[1,20,4,256]{3,1,2,0:T(8,128)(2,1)S(1)}, u32[]{:S(2)}, u32[]{:S(2)}) collective-permute-start(bf16[1,20,4,256]{3,1,2,0:T(8,128)(2,1)} %copy.500), channel_id=1, source_target_pairs={{0,8},{8,16},{16,24},{24,32},{32,40},{40,48},{48,56},{56,64},{64,7... | collective-permute-start | bytes 122888 | tf_op jit(solution)/shard_map/ppermute | solution.py:25
  8.8 19.2 %collective-permute-start.1 = (bf16[1,20,4,256]{3,1,2,0:T(8,128)(2,1)}, bf16[1,20,4,256]{3,1,2,0:T(8,128)(2,1)S(1)}, u32[]{:S(2)}, u32[]{:S(2)}) collective-permute-start(bf16[1,20,4,256]{3,1,2,0:T(8,128)(2,1)} %copy.501), channel_id=1, source_target_pairs={{8,0},{16,8},{24,16},{32,24},{40,32},{48,40},{56,48},{64,56},{72,6... | collective-permute-start | bytes 122888 | tf_op jit(solution)/shard_map/ppermute | solution.py:26
  15.0 7.2 copy-start.11
  15.0 7.2 copy-start.13
  15.0 10.1 copy-start.20
  15.0 10.8 copy-start.21
  15.0 12.1 %copy-start.10 = (bf16[2,20,180]{2,0,1:T(2,128)(2,1)S(1)}, bf16[2,20,180]{2,0,1:T(2,128)(2,1)}, u32[]{:S(2)}) copy-start(bf16[2,20,180]{2,0,1:T(2,128)(2,1)} %param.8) | copy-start | bytes 43204
  15.0 12.2 %copy-start.1 = (bf16[1,20,128,256]{3,2,1,0:T(8,128)(2,1)S(1)}, bf16[1,20,128,256]{3,2,1,0:T(8,128)(2,1)}, u32[]{:S(2)}) copy-start(bf16[1,20,128,256]{3,2,1,0:T(8,128)(2,1)} %param.6) | copy-start | bytes 3932164
  22.1 233.8 %all-reduce.7.cloned.1.call-start = ((), (), s32[]{:S(2)}) async-start(), calls=%async_computation.1 | async-start | bytes 655360 | tf_op jit(solution)/shard_map/psum | solution.py:113
  28.0 1.2 copy-start
  30.2 9.5 collective-permute-start.2
  32.4 7.8 collective-permute-start.3
  65.8 3.8 copy-start.16
  95.1 4.3 copy-start.6
  101.7 8.9 slice-start
  101.7 8.9 slice-start.1
  104.2 6.4 slice-start.2
  110.6 2.4 copy-start.4
  123.5 584.3 %all-reduce.9.cloned.1.call-start = ((), (), s32[]{:S(2)}) async-start(), calls=%async_computation.2 | async-start | bytes 655360 | tf_op jit(solution)/shard_map/psum | solution.py:113
  128.0 469.0 %copy-start.5 = (f32[32,256]{1,0:T(8,128)S(1)}, f32[32,256]{1,0:T(8,128)}, u32[]{:S(2)}) copy-start(f32[32,256]{1,0:T(8,128)} %get-tuple-element.296) | copy-start | bytes 98308
  590.4 9.0 copy-start.2
  597.0 12.7 %copy-start.12 = (bf16[256,32]{0,1:T(8,128)(2,1)S(1)}, bf16[256,32]{0,1:T(8,128)(2,1)}, u32[]{:S(2)}) copy-start(bf16[256,32]{0,1:T(8,128)(2,1)} %copy-done.11) | copy-start | bytes 49156
  597.1 12.7 %copy-start.14 = (bf16[256,32]{0,1:T(8,128)(2,1)S(1)}, bf16[256,32]{0,1:T(8,128)(2,1)}, u32[]{:S(2)}) copy-start(bf16[256,32]{0,1:T(8,128)(2,1)} %copy-done.13) | copy-start | bytes 49156
  612.9 7.1 collective-permute-start.4
  612.9 7.0 collective-permute-start.5
  621.7 6.2 collective-permute-start.6
  622.2 6.0 collective-permute-start.7
  627.4 215.2 %all-reduce.11.cloned.1.call-start = ((), (), s32[]{:S(2)}) async-start(), calls=%async_computation.3 | async-start | bytes 655360 | tf_op jit(solution)/shard_map/psum | solution.py:113
  644.8 3.2 copy-start.19
  664.2 11.1 copy-start.8
  671.8 3.3 copy-start.17
  671.8 8.0 copy-start.15
  679.8 9.6 copy-start.18
  694.6 5.3 copy-start.9
  702.5 141.3 %copy-start.3 = (f32[20,20,16]{1,2,0:T(8,128)S(1)}, f32[20,20,16]{1,2,0:T(8,128)}, u32[]{:S(2)}) copy-start(f32[20,20,16]{1,2,0:T(8,128)} %get-tuple-element.285) | copy-start | bytes 76804
Sparse Core Ops, SparseCore 0:
  22.2 73.9 all-reduce.4
  123.6 132.2 all-reduce.6
  627.6 72.3 all-reduce.8
  707.9 134.6 all-reduce.10
